TPU v7x, 32 devices: a whole 2x2x4 slice. The times are simulated.
32 devices in a mesh: dp: 4 (over x, core), ctx: 4 (over z), tensor: 2 (over y).
Axes of the slice: x: 2, y: 2, z: 4, core: 2. Of those that a mesh axis runs over, the one named last changes fastest.
Arguments:
- inputs: bfloat16 [8192, 768], P(('dp', 'ctx')), may hold values from -6 to 6
- segments: int32 [4, 2048], P('dp', 'ctx'), may hold values from 0 to 7, never falling along the last dimension, each value on 1 to 1536 neighbouring positions
- query_proj: bfloat16 [768, 768], P(None, 'tensor'), may hold values from -0.4375 to 0.4375
- key_proj: bfloat16 [768, 768], P(None, 'tensor'), may hold values from -0.21875 to 0.21875
- value_proj: bfloat16 [768, 768], P(None, 'tensor'), may hold values from -0.21875 to 0.21875
- query_bias: bfloat16 [768], P('tensor'), may hold values from -3 to 3
- value_bias: bfloat16 [768], P('tensor'), may hold values from -0.59765625 to 0.59765625
- output_proj: bfloat16 [768, 768], P('tensor'), may hold values from -0.875 to 0.875
- output_bias: bfloat16 [768], replicated, may hold values from -1.1953125 to 1.1953125
- attn_gain: bfloat16 [768], replicated, may hold values from 0.5 to 1.5
- attn_shift: bfloat16 [768], replicated, may hold values from -1.1953125 to 1.1953125
- expand_proj: bfloat16 [768, 3072], P(None, 'tensor'), may hold values from -0.21875 to 0.21875
- expand_bias: bfloat16 [3072], P('tensor'), may hold values from -3 to 3
- shrink_proj: bfloat16 [3072, 768], P('tensor'), may hold values from -0.109375 to 0.109375
- shrink_bias: bfloat16 [768], replicated, may hold values from -1.1953125 to 1.1953125
- final_gain: bfloat16 [768], replicated, may hold values from 0.5 to 1.5
- final_shift: bfloat16 [768], replicated, may hold values from -1.1953125 to 1.1953125
- cotangent: bfloat16 [8192, 768], P(('dp', 'ctx')), may hold values from -6 to 6
Outputs:
- output: bfloat16 [8192, 768], P(('dp', 'ctx'))
- input_grad: float32 [8192, 768], P(('dp', 'ctx'))
- query_grad: float32 [768, 768], P(None, 'tensor')
- key_grad: float32 [768, 768], P(None, 'tensor')
- value_grad: float32 [768, 768], P(None, 'tensor')
- qbias_grad: float32 [768], P('tensor')
- vbias_grad: float32 [768], P('tensor')
- oproj_grad: float32 [768, 768], P('tensor')
- obias_grad: float32 [768], replicated
- again_grad: float32 [768], replicated
- ashift_grad: float32 [768], replicated
- expand_grad: float32 [768, 3072], P(None, 'tensor')
- ebias_grad: float32 [3072], P('tensor')
- shrink_grad: float32 [3072, 768], P('tensor')
- sbias_grad: float32 [768], replicated
- fgain_grad: float32 [768], replicated
- fshift_grad: float32 [768], replicated
Inputs may be any that keep to these rules, and one draw needn't show every extreme that they name: `segments`: along each sequence the ids never fall; every id from 0 to 7 names one document of the sequence, and one document has 1536 tokens.
All inputs are finite; a program needn't handle non-finite values.
Results may differ from a plain program's by a relative error of at most 0.019.
Values may be sent and summed in bfloat16 or wider, within the bound.
A program may use at most 256 MiB of HBM per device.

v0:
```python
import jax
import jax.numpy as jnp
from jax import lax
from jax.sharding import PartitionSpec as P

HEAD_DIM = 64
norm_eps = 1e-12
masked = -1e30
contract_rows = (((0,), (0,)), ((), ()))
contract_cols = (((1,), (1,)), ((), ()))


def matmul(left, right):
    return jnp.dot(left, right, preferred_element_type=jnp.float32)


def inner_rows(left, right):
    return lax.dot_general(left, right, contract_rows, preferred_element_type=jnp.float32)


def inner_cols(left, right):
    return lax.dot_general(left, right, contract_cols, preferred_element_type=jnp.float32)


def norm_forward(values, gain, shift):
    centred = values - jnp.mean(values, axis=-1, keepdims=True)
    spread = jnp.mean(centred * centred, axis=-1, keepdims=True)
    recip = lax.rsqrt(spread + norm_eps)
    normed = centred * recip
    return (normed * gain + shift, normed, recip)


def norm_backward(upstream, normed, recip, gain):
    scaled = upstream * gain
    centred = (
        scaled
        - jnp.mean(scaled, axis=-1, keepdims=True)
        - normed * jnp.mean(scaled * normed, axis=-1, keepdims=True)
    )
    return (centred * recip, jnp.sum(upstream * normed, axis=0), jnp.sum(upstream, axis=0))


def cross_scores(left, right):
    return inner_cols(left, right)


def spread_apply(weights_in, right):
    return matmul(weights_in, right)


def spread_transpose(weights_in, left):
    return inner_rows(weights_in, left)


def body(
    inputs,
    segments,
    query_proj,
    key_proj,
    value_proj,
    query_bias,
    value_bias,
    output_proj,
    output_bias,
    attn_gain,
    attn_shift,
    expand_proj,
    expand_bias,
    shrink_proj,
    shrink_bias,
    final_gain,
    final_shift,
    cotangent,
):
    head_count = query_proj.shape[1] // HEAD_DIM
    scale = HEAD_DIM ** (-0.5)
    seg_local = segments[0]
    queries = (matmul(inputs, query_proj) + query_bias.astype(jnp.float32)).astype(jnp.bfloat16)
    keys = matmul(inputs, key_proj).astype(jnp.bfloat16)
    values = (matmul(inputs, value_proj) + value_bias.astype(jnp.float32)).astype(jnp.bfloat16)
    all_keys, all_values, key_ids = (
        lax.all_gather(keys, "ctx", axis=0, tiled=True),
        lax.all_gather(values, "ctx", axis=0, tiled=True),
        lax.all_gather(seg_local.astype(jnp.bfloat16), "ctx", axis=0, tiled=True),
    )
    query_segs = seg_local.astype(jnp.float32)
    key_segs = key_ids.astype(jnp.float32)
    same_seg = query_segs[:, None] == key_segs[None, :]

    def split_heads(matrix):
        return jnp.swapaxes(matrix.reshape(matrix.shape[0], head_count, HEAD_DIM), 0, 1)

    def join_heads(stack):
        return jnp.swapaxes(stack, 0, 1).reshape(stack.shape[1], head_count * HEAD_DIM)

    query_heads = split_heads(queries)
    key_heads = split_heads(all_keys)
    value_heads = split_heads(all_values)

    def head_forward(state, triple):
        query_head, key_head, value_head = triple
        scores = cross_scores(query_head, key_head) * scale
        scores = jnp.where(same_seg, scores, masked)
        row_max = jnp.max(scores, axis=1, keepdims=True)
        exp_scores = jnp.where(same_seg, jnp.exp(scores - row_max), 0.0)
        row_sum = jnp.sum(exp_scores, axis=1, keepdims=True)
        attn_probs = (exp_scores / row_sum).astype(jnp.bfloat16)
        mixed = spread_apply(attn_probs, value_head)
        return (state, (mixed, row_max + jnp.log(row_sum)))

    mixed_heads, log_sums = lax.scan(head_forward, None, (query_heads, key_heads, value_heads))[1]
    attended = join_heads(mixed_heads).astype(jnp.bfloat16)
    attn_total = lax.psum(matmul(attended, output_proj).astype(jnp.bfloat16), "tensor").astype(
        jnp.float32
    )
    attn_gain_f = attn_gain.astype(jnp.float32)
    first, first_normed, first_recip = norm_forward(
        inputs.astype(jnp.float32) + attn_total + output_bias.astype(jnp.float32),
        attn_gain_f,
        attn_shift.astype(jnp.float32),
    )
    first_low = first.astype(jnp.bfloat16)
    pre_act = matmul(first_low, expand_proj) + expand_bias.astype(jnp.float32)
    activated, gelu_back = jax.vjp(lambda pre_in: jax.nn.gelu(pre_in, approximate=False), pre_act)
    hidden = activated.astype(jnp.bfloat16)
    feed_total = lax.psum(matmul(hidden, shrink_proj).astype(jnp.bfloat16), "tensor").astype(
        jnp.float32
    )
    second = first + feed_total + shrink_bias.astype(jnp.float32)
    final_gain_f = final_gain.astype(jnp.float32)
    output, second_normed, second_recip = norm_forward(
        second, final_gain_f, final_shift.astype(jnp.float32)
    )
    upstream = cotangent.astype(jnp.float32)
    grad_second, fgain_grad, fshift_grad = norm_backward(
        upstream, second_normed, second_recip, final_gain_f
    )
    sbias_grad = jnp.sum(grad_second, axis=0)
    grad_second_low = grad_second.astype(jnp.bfloat16)
    shrink_grad = inner_rows(hidden, grad_second_low)
    grad_act = inner_cols(grad_second_low, shrink_proj)
    grad_pre = gelu_back(grad_act)[0].astype(jnp.bfloat16)
    ebias_grad = jnp.sum(grad_pre.astype(jnp.float32), axis=0)
    expand_grad = inner_rows(first_low, grad_pre)
    grad_first = grad_second + lax.psum(
        inner_cols(grad_pre, expand_proj).astype(jnp.bfloat16), "tensor"
    ).astype(jnp.float32)
    grad_mix, again_grad, ashift_grad = norm_backward(
        grad_first, first_normed, first_recip, attn_gain_f
    )
    obias_grad = jnp.sum(grad_mix, axis=0)
    grad_mix_low = grad_mix.astype(jnp.bfloat16)
    oproj_grad = inner_rows(attended, grad_mix_low)
    grad_attended = inner_cols(grad_mix_low, output_proj).astype(jnp.bfloat16)
    grad_heads = split_heads(grad_attended)

    def head_backward(state, group):
        query_head, key_head, value_head, grad_head, log_sum = group
        scores = cross_scores(query_head, key_head) * scale
        attn_probs = jnp.where(same_seg, jnp.exp(scores - log_sum), 0.0)
        grad_probs = cross_scores(grad_head, value_head)
        row_dot = jnp.sum(attn_probs * grad_probs, axis=1, keepdims=True)
        grad_scores = (attn_probs * (grad_probs - row_dot)).astype(jnp.bfloat16)
        grad_query = spread_apply(grad_scores, key_head) * scale
        grad_key = spread_transpose(grad_scores, query_head) * scale
        grad_value = spread_transpose(attn_probs.astype(jnp.bfloat16), grad_head)
        return (state, (grad_query, grad_key, grad_value))

    query_back, key_back, value_back = lax.scan(
        head_backward, None, (query_heads, key_heads, value_heads, grad_heads, log_sums)
    )[1]
    grad_queries = join_heads(query_back).astype(jnp.bfloat16)
    key_sum, value_sum = (
        lax.psum_scatter(
            join_heads(key_back).astype(jnp.bfloat16), "ctx", scatter_dimension=0, tiled=True
        ).astype(jnp.float32),
        lax.psum_scatter(
            join_heads(value_back).astype(jnp.bfloat16), "ctx", scatter_dimension=0, tiled=True
        ).astype(jnp.float32),
    )
    grad_keys = key_sum.astype(jnp.bfloat16)
    grad_values = value_sum.astype(jnp.bfloat16)
    qbias_grad = jnp.sum(grad_queries.astype(jnp.float32), axis=0)
    vbias_grad = jnp.sum(grad_values.astype(jnp.float32), axis=0)
    query_grad = inner_rows(inputs, grad_queries)
    key_grad = inner_rows(inputs, grad_keys)
    value_grad = inner_rows(inputs, grad_values)
    back_terms = (
        inner_cols(grad_queries, query_proj)
        + inner_cols(grad_keys, key_proj)
        + inner_cols(grad_values, value_proj)
    )
    input_grad = grad_mix + lax.psum(back_terms.astype(jnp.bfloat16), "tensor").astype(jnp.float32)
    (
        query_grad,
        key_grad,
        value_grad,
        qbias_grad,
        vbias_grad,
        oproj_grad,
        obias_grad,
        again_grad,
        ashift_grad,
        expand_grad,
        ebias_grad,
        shrink_grad,
        sbias_grad,
        fgain_grad,
        fshift_grad,
    ) = lax.psum(
        (
            query_grad,
            key_grad,
            value_grad,
            qbias_grad,
            vbias_grad,
            oproj_grad,
            obias_grad,
            again_grad,
            ashift_grad,
            expand_grad,
            ebias_grad,
            shrink_grad,
            sbias_grad,
            fgain_grad,
            fshift_grad,
        ),
        ("dp", "ctx"),
    )
    return (
        output.astype(jnp.bfloat16),
        input_grad,
        query_grad,
        key_grad,
        value_grad,
        qbias_grad,
        vbias_grad,
        oproj_grad,
        obias_grad,
        again_grad,
        ashift_grad,
        expand_grad,
        ebias_grad,
        shrink_grad,
        sbias_grad,
        fgain_grad,
        fshift_grad,
    )


def solution(mesh):
    in_specs = (
        P(("dp", "ctx"), None),
        P("dp", "ctx"),
        P(None, "tensor"),
        P(None, "tensor"),
        P(None, "tensor"),
        P("tensor"),
        P("tensor"),
        P("tensor", None),
        P(),
        P(),
        P(),
        P(None, "tensor"),
        P("tensor"),
        P("tensor", None),
        P(),
        P(),
        P(),
        P(("dp", "ctx"), None),
    )
    out_specs = (
        P(("dp", "ctx"), None),
        P(("dp", "ctx"), None),
        P(None, "tensor"),
        P(None, "tensor"),
        P(None, "tensor"),
        P("tensor"),
        P("tensor"),
        P("tensor", None),
        P(),
        P(),
        P(),
        P(None, "tensor"),
        P("tensor"),
        P("tensor", None),
        P(),
        P(),
        P(),
    )
    return jax.shard_map(body, mesh=mesh, in_specs=in_specs, out_specs=out_specs, check_vma=False)
```

profile of v0, /device:TPU:0, one launch (start us, length us, event | category | flops | bytes accessed | tf_op | source)
XLA Modules:
  0.0 743.4 jit_solution(2113761524882374570)
XLA Ops:
  7.3 2.8 convolution_convert_fusion.4
  10.2 2.4 fusion.62
  12.7 13.7 %all-gather = bf16[1,2048]{1,0:T(2,128)(2,1)S(1)} all-gather(bf16[1,512]{1,0:T(2,128)(2,1)S(1)} %get-tuple-element.288), channel_id=2, replica_groups=mesh['dp'=4,'ctx'=4,'tensor'=2] {'ctx'}, dimensions={1}, use_global_device_ids=true | all-gather | bytes 5120 | tf_op jit(solution)/shard_map/all_gather | solution.py:84
  29.1 21.0 %all-gather.4.cloned.1.call-done = bf16[2048,384]{1,0:T(8,128)(2,1)} async-done(((bf16[512,384]{1,0:T(8,128)(2,1)}), bf16[2048,384]{1,0:T(8,128)(2,1)}) %all-gather.4.cloned.1.call-update) | async-done | bytes 1572880 | tf_op jit(solution)/shard_map/all_gather | solution.py:82
  50.1 2.6 copy.43
  52.6 4.1 copy.45
  56.8 31.5 %all-gather.6.cloned.1.call-done = bf16[2048,384]{1,0:T(8,128)(2,1)} async-done(((bf16[512,384]{1,0:T(8,128)(2,1)}), bf16[2048,384]{1,0:T(8,128)(2,1)}) %all-gather.6.cloned.1.call-update) | async-done | bytes 1572880 | tf_op jit(solution)/shard_map/all_gather | solution.py:83
  88.2 2.6 copy.44
  90.8 4.1 copy.46
  94.9 38.4 %while.28 = (s32[]{:T(128)}, bf16[6,512,64]{1,2,0:T(8,128)(2,1)S(1)}, f32[6,512,1]{1,2,0:T(1,128)}, bf16[6,512,64]{2,1,0:T(8,128)(2,1)}, bf16[6,2048,64]{2,1,0:T...) while((s32[]{:T(128)}, ...), condition=%wide.region_3.4_spmd.clone, body=%wide.region_0.3_spmd.clone.sunk | while | flops 286260736 | bytes 13946985 | solution.py:111
  98.1 2.6 fusion.134
  104.5 2.6 fusion.134
  110.9 2.6 fusion.134
  117.3 2.6 fusion.134
  123.7 2.6 fusion.134
  130.1 2.6 fusion.134
  133.3 2.7 convolution_convert_fusion.2
  140.6 28.8 %all-reduce.8.cloned.1.call-done = bf16[512,768]{1,0:T(8,128)(2,1)} async-done(((bf16[512,768]{1,0:T(8,128)(2,1)}), bf16[512,768]{1,0:T(8,128)(2,1)}) %all-reduce.8.cloned.1.call-update) | async-done | bytes 786448 | tf_op jit(solution)/shard_map/psum | solution.py:113
  171.5 9.5 %multiply_convert_fusion.1 = (bf16[512,1536]{1,0:T(8,128)(2,1)S(1)}, f32[512,1536]{1,0:T(8,128)}, f32[512,1536]{1,0:T(8,128)}) fusion(f32[1536]{0:T(1024)S(1)} %copy-done.41, bf16[768,1536]{1,0:T(8,128)(2,1)S(1)} %copy-done, f32[768]{0:T(1024)S(1)} %copy-done.38, f32[768]{0:T(1024)S(1)} %copy-done.23, f32[512]{0:T(512)S(1)} %add_rsqrt_fusion.1, ...), kind=kOutput, calls=%fused_computation.62 | convolution fusion | flops 1263403008 | bytes 11815936 | tf_op jit(solution)/shard_map/dot_general | solution.py:14
  182.3 2.3 convolution_convert_fusion.1
  184.8 34.2 %all-reduce.10.cloned.1.call-done = bf16[512,768]{1,0:T(8,128)(2,1)} async-done(((bf16[512,768]{1,0:T(8,128)(2,1)}), bf16[512,768]{1,0:T(8,128)(2,1)}) %all-reduce.10.cloned.1.call-update) | async-done | bytes 786448 | tf_op jit(solution)/shard_map/psum | solution.py:126
  219.1 2.2 fusion.78
  225.0 2.9 convert_reduce_fusion
  229.1 2.3 convolution_convert_fusion
  231.5 34.4 %all-reduce.12.cloned.1.call-done = bf16[512,768]{1,0:T(8,128)(2,1)} async-done(((bf16[512,768]{1,0:T(8,128)(2,1)}), bf16[512,768]{1,0:T(8,128)(2,1)}) %all-reduce.12.cloned.1.call-update) | async-done | bytes 786448 | tf_op jit(solution)/shard_map/psum | solution.py:145
  265.9 3.5 multiply_reduce_fusion.1
  273.7 70.0 %while.29 = (s32[]{:T(128)}, bf16[6,512,64]{1,2,0:T(8,128)(2,1)S(1)}, bf16[6,2048,64]{1,2,0:T(8,128)(2,1)}, bf16[6,2048,64]{1,2,0:T(8,128)(2,1)}, bf16[6,512,64]...) while((s32[]{:T(128)}, ...), condition=%wide.region_17.18_spmd.clone, body=%wide.region_15.17_spmd.clone.sunk | while | flops 681737728 | bytes 34759808 | solution.py:169
  276.2 2.6 multiply_reduce_fusion.7
  287.9 2.6 multiply_reduce_fusion.7
  299.5 2.6 multiply_reduce_fusion.7
  302.6 2.2 fusion.146
  311.2 2.6 multiply_reduce_fusion.7
  322.9 2.6 multiply_reduce_fusion.7
  325.9 2.2 fusion.146
  334.5 2.6 multiply_reduce_fusion.7
  345.1 5.1 fusion.67
  350.3 3.8 fusion.73
  357.4 21.8 %reduce-scatter.3.cloned.1.call-done = bf16[512,384]{0,1:T(8,128)(2,1)} async-done(((bf16[2048,384]{0,1:T(8,128)(2,1)}), bf16[512,384]{0,1:T(8,128)(2,1)}) %reduce-scatter.3.cloned.1.call-update) | async-done | bytes 393232 | tf_op jit(solution)/shard_map/reduce_scatter | solution.py:174
  379.1 3.0 fusion.82
  382.1 33.8 %reduce-scatter.5.cloned.1.call-done = bf16[512,384]{0,1:T(8,128)(2,1)} async-done(((bf16[2048,384]{0,1:T(8,128)(2,1)}), bf16[512,384]{0,1:T(8,128)(2,1)}) %reduce-scatter.5.cloned.1.call-update) | async-done | bytes 393232 | tf_op jit(solution)/shard_map/reduce_scatter | solution.py:177
  415.8 3.5 add_convert_fusion.1
  424.7 61.2 %all-reduce = (f32[384]{0:T(512)}, f32[384]{0:T(512)}, f32[768]{0:T(1024)}, f32[768]{0:T(1024)}, f32[768]{0:T(1024)}, /*index=5*/f32[1536]{0:T(1024)}, f32[768]{0:T(1024)}, f32[768]{0:T(1024)}, f32[768]{0:T(1024)}) all-reduce(f32[384]{0:T(512)S(1)} %reduce_sum.182, ...), channel_id=1, replica_groups=mesh['dp'=4,'ctx'=4,'tensor'=2] {'dp','ctx'}, use_global_device_ids=true, to_apply=%region_25.26 | all-reduce | flops 6912 | bytes 55296 | tf_op jit(solution)/shard_map/psum | solution.py:210
  485.9 2.4 convert_add_fusion
  488.3 231.7 %all-reduce.16.cloned.1.call-done = (f32[768,384]{0,1:T(8,128)}, f32[768,384]{0,1:T(8,128)}, f32[768,384]{0,1:T(8,128)}, f32[384,768]{1,0:T(8,128)}, f32[768,1536]{1,0:T(8,128)}, /*index=5*/f32[1536,768]{1,0:T(8,128)}) async-done(((f32[768,384]{0,1:T(8,128)}, f32[768,384]{0,1:T(8,128)}, f32[768,384]{0,1:T(8,128)}, f32[384,768]{1,0:T(8,128)}, f32[768,1536]{1,0:T(8,128)}, /*index=5*/f32[1536,768]{1,0:T(8,128)}), ...) | async-done | bytes 14155792 | tf_op jit(solution)/shard_map/psum | solution.py:210
  720.1 2.7 copy.50
  722.8 2.7 copy.51
  728.0 5.5 copy.92
  733.5 2.4 copy.93
  (235 shorter events, 106.0 us)
Async XLA Ops:
  7.2 164.2 %copy-start = (bf16[768,1536]{1,0:T(8,128)(2,1)S(1)}, bf16[768,1536]{1,0:T(8,128)(2,1)}, u32[]{:S(2)}) copy-start(bf16[768,1536]{1,0:T(8,128)(2,1)} %param.33) | copy-start | bytes 7077892
  7.2 3.0 copy-start.2
  7.2 2.9 copy-start.47
  7.2 5.4 copy-start.48
  7.2 5.4 copy-start.43
  7.2 42.8 %all-gather.4.cloned.1.call-start = ((), (), s32[]{:S(2)}) async-start(), calls=%async_computation.2 | async-start | bytes 1966080 | tf_op jit(solution)/shard_map/all_gather | solution.py:82
  10.1 78.1 %all-gather.6.cloned.1.call-start = ((), (), s32[]{:S(2)}) async-start(), calls=%async_computation.3 | async-start | bytes 1966080 | tf_op jit(solution)/shard_map/all_gather | solution.py:83
  12.6 156.8 %all-reduce.8.cloned.1.call-start = ((), (), s32[]{:S(2)}) async-start(), calls=%async_computation.4 | async-start | bytes 1572864 | tf_op jit(solution)/shard_map/psum | solution.py:113
  133.3 38.1 %copy-start.12 = (bf16[6,512,64]{1,2,0:T(8,128)(2,1)}, bf16[6,512,64]{1,2,0:T(8,128)(2,1)S(1)}, u32[]{:S(2)}) copy-start(bf16[6,512,64]{1,2,0:T(8,128)(2,1)S(1)} %get-tuple-element.109) | copy-start | bytes 1179652
  136.0 83.0 %all-reduce.10.cloned.1.call-start = ((), (), s32[]{:S(2)}) async-start(), calls=%async_computation.5 | async-start | bytes 1572864 | tf_op jit(solution)/shard_map/psum | solution.py:126
  169.4 2.1 copy-start.41
  170.9 10.1 %copy-start.26 = (f32[512]{0:T(512)}, f32[512]{0:T(512)S(1)}, u32[]{:S(2)}) copy-start(f32[512]{0:T(512)S(1)} %broadcast_multiply_fusion.5) | copy-start | bytes 6148
  171.5 9.6 %copy-start.29 = (f32[512]{0:T(512)}, f32[512]{0:T(512)S(1)}, u32[]{:S(2)}) copy-start(f32[512]{0:T(512)S(1)} %add_rsqrt_fusion.1) | copy-start | bytes 6148
  171.5 10.7 %copy-start.49 = (bf16[1536,768]{1,0:T(8,128)(2,1)S(1)}, bf16[1536,768]{1,0:T(8,128)(2,1)}, u32[]{:S(2)}) copy-start(bf16[1536,768]{1,0:T(8,128)(2,1)} %param.35) | copy-start | bytes 7077892
  182.2 2.6 copy-start.44
  182.2 2.6 copy-start.45
  182.2 2.6 copy-start.46
  182.2 36.8 %copy-start.24 = (f32[768]{0:T(1024)S(1)}, f32[768]{0:T(1024)}, u32[]{:S(2)}) copy-start(f32[768]{0:T(1024)} %convert_element_type.185) | copy-start | bytes 9220
  182.2 36.8 %copy-start.27 = (f32[512]{0:T(512)S(1)}, f32[512]{0:T(512)}, u32[]{:S(2)}) copy-start(f32[512]{0:T(512)} %copy-done.26) | copy-start | bytes 6148
  182.2 36.8 %copy-start.30 = (f32[512]{0:T(512)S(1)}, f32[512]{0:T(512)}, u32[]{:S(2)}) copy-start(f32[512]{0:T(512)} %copy-done.29) | copy-start | bytes 6148
  182.2 36.8 %copy-start.39 = (f32[768]{0:T(1024)S(1)}, f32[768]{0:T(1024)}, u32[]{:S(2)}) copy-start(f32[768]{0:T(1024)} %convert_element_type.186) | copy-start | bytes 9220
  184.5 81.4 %all-reduce.12.cloned.1.call-start = ((), (), s32[]{:S(2)}) async-start(), calls=%async_computation.6 | async-start | bytes 1572864 | tf_op jit(solution)/shard_map/psum | solution.py:145
  219.0 2.6 copy-start.14
  221.3 3.4 copy-start.54
  221.6 3.1 copy-start.53
  224.7 3.2 copy-start.3
  231.4 38.0 %copy-start.4 = (f32[512,768]{1,0:T(8,128)S(1)}, f32[512,768]{1,0:T(8,128)}, u32[]{:S(2)}) copy-start(f32[512,768]{1,0:T(8,128)} %copy-done.3) | copy-start | bytes 4718596
  231.4 38.0 %copy-start.9 = (bf16[512,768]{1,0:T(8,128)(2,1)S(1)}, bf16[512,768]{1,0:T(8,128)(2,1)}, u32[]{:S(2)}) copy-start(bf16[512,768]{1,0:T(8,128)(2,1)} %all-reduce.8.cloned.1.call-done) | copy-start | bytes 2359300
  231.4 147.7 %reduce-scatter.3.cloned.1.call-start = ((), (), s32[]{:S(2)}) async-start(), calls=%async_computation.7 | async-start | bytes 1966080 | tf_op jit(solution)/shard_map/reduce_scatter | solution.py:174
  265.9 3.6 copy-start.15
  269.5 2.5 copy-start.17
  343.7 72.2 %reduce-scatter.5.cloned.1.call-start = ((), (), s32[]{:S(2)}) async-start(), calls=%async_computation.8 | async-start | bytes 1966080 | tf_op jit(solution)/shard_map/reduce_scatter | solution.py:177
  344.4 5.8 copy-start.10
  344.4 5.8 copy-start.25
  344.5 5.8 copy-start.28
  344.5 5.7 copy-start.31
  344.5 141.4 %all-reduce.14.cloned.1.call-start = ((), (), s32[]{:S(2)}) async-start(), calls=%async_computation.9 | async-start | bytes 1572864 | tf_op jit(solution)/shard_map/psum | solution.py:193
  345.1 5.2 copy-start.40
  345.1 5.2 copy-start.52
  350.2 3.9 copy-start.22
  357.4 58.5 %copy-start.21 = (bf16[768,384]{1,0:T(8,128)(2,1)S(1)}, bf16[768,384]{1,0:T(8,128)(2,1)}, u32[]{:S(2)}) copy-start(bf16[768,384]{1,0:T(8,128)(2,1)} %param.26) | copy-start | bytes 1769476
  419.4 3.0 copy-start.18
  419.4 300.7 %all-reduce.16.cloned.1.call-start = ((), (), s32[]{:S(2)}) async-start(), calls=%async_computation.10 | async-start | bytes 28311552 | tf_op jit(solution)/shard_map/psum | solution.py:210
  720.1 5.5 copy-start.20
  722.8 4.1 copy-start.19
  727.0 6.5 slice-start
  728.0 5.5 slice-start.1
  733.5 3.4 copy-start.1
  (18 other events, 22.7 us)
Sparse Core Ops, SparseCore 0:
  10.2 39.8 all-gather.3
  52.2 35.9 all-gather.5
  136.1 33.1 all-reduce.7
  184.7 34.3 all-reduce.9
  231.5 34.3 all-reduce.11
  343.8 35.2 reduce-scatter.2
  381.5 34.2 reduce-scatter.4
  419.5 33.2 all-reduce.13
  459.1 260.8 all-reduce.15
where the time goes:
time: 746 us; the launch traced here: 743 us
  waiting for transfers between devices  438 us (59%)
  matrix products  141 us (19%)
  blocking collectives  74.9 us (10%)
  local copies, waits for them, and re-layouts  44.8 us (6%)
  other arithmetic  29.9 us (4%)
  between operations  14.4 us (2%)
    psum x1, waiting for transfers between devices, body(): lax.psum((query_grad, key_grad, value_grad, qbias_grad, vbias_grad, oproj...  232 us
    psum x1, blocking collectives, body(): lax.psum((query_grad, key_grad, value_grad, qbias_grad, vbias_grad, oproj...  61.2 us
    dot_general x24, matrix products, inner_cols(): lax.dot_general(left, right, contract_cols, preferred_element_type=jnp.fl...  52.3 us
    dot_general x18, matrix products, matmul(): return jnp.dot(left, right, preferred_element_type=jnp.float32)  47.6 us
    dot_general x18, matrix products, inner_rows(): lax.dot_general(left, right, contract_rows, preferred_element_type=jnp.fl...  40.7 us
    psum x1, waiting for transfers between devices, body(): lax.psum(inner_cols(grad_pre, expand_proj).astype(jnp.bfloat16), 'tensor')  34.4 us
    psum x1, waiting for transfers between devices, body(): lax.psum(matmul(hidden, shrink_proj).astype(jnp.bfloat16), 'tensor')  34.2 us
    reduce_scatter x1, waiting for transfers between devices, body(): lax.psum_scatter(join_heads(value_back).astype(jnp.bfloat16), 'ctx', scat...  33.8 us
  transfers between devices with their start and end apart: 9, of which 8 were waited for; matrix products, arithmetic and copies ran while one was open for 5% of the time, Pallas kernels for 0%

commit v1 on v0

--- a/solution.py
+++ b/solution.py
@@ -1,3 +1,4 @@
+import functools
 import jax
 import jax.numpy as jnp
 from jax import lax
@@ -8,6 +9,13 @@
 masked = -1e30
 contract_rows = (((0,), (0,)), ((), ()))
 contract_cols = (((1,), (1,)), ((), ()))
+
+
+def use_plane(mine, axis_id, mesh_ax):
+    return lax.psum(lax.psum(mine, axis_name=mesh_ax), axis_name=axis_id)
+
+
+pack_page = functools.partial(use_plane, axis_id="dp", mesh_ax="ctx")
 
 
 def matmul(left, right):
@@ -207,7 +215,7 @@
         sbias_grad,
         fgain_grad,
         fshift_grad,
-    ) = lax.psum(
+    ) = pack_page(
         (
             query_grad,
             key_grad,
@@ -224,8 +232,7 @@
             sbias_grad,
             fgain_grad,
             fshift_grad,
-        ),
-        ("dp", "ctx"),
+        )
     )
     return (
         output.astype(jnp.bfloat16),

time: 746 us -> 1210 us (1.62)
  waiting for transfers between devices: 438 us -> 939 us
  blocking collectives: 74.9 us -> 42 us
    psum x1 -> x2, waiting for transfers between devices: 232 us -> 726 us  [use_plane(): return lax.psum(lax.psum(mine, axis_name=mesh_ax), axis_name=axis_id)]
    psum x1 -> x2, blocking collectives: 61.2 us -> 28.4 us  [use_plane(): return lax.psum(lax.psum(mine, axis_name=mesh_ax), axis_name=axis_id)]
    reduce_scatter x1, waiting for transfers between devices: 21.8 us -> 34.2 us  [body(): lax.psum_scatter(join_heads(key_back).astype(jnp.bfloat16), 'ctx', scatte...]
    unnamed x122 -> x124, local copies, waits for them, and re-layouts: 29.6 us -> 30.2 us
  transfers between devices with their start and end apart: 9 -> 10, of which waited for: 8 -> 10; matrix products, arithmetic and copies ran while one was open for 5% -> 3% of each run, Pallas kernels for 0% -> 0%
where the time goes in v1:
time: 1210 us
  waiting for transfers between devices  939 us (78%)
  matrix products  138 us (11%)
  local copies, waits for them, and re-layouts  45.4 us (4%)
  blocking collectives  42 us (3%)
  other arithmetic  29.9 us (2%)
  between operations  14.9 us (1%)
    psum x2, waiting for transfers between devices, use_plane(): return lax.psum(lax.psum(mine, axis_name=mesh_ax), axis_name=axis_id)  726 us
    dot_general x24, matrix products, inner_cols(): lax.dot_general(left, right, contract_cols, preferred_element_type=jnp.fl...  48 us
    dot_general x18, matrix products, matmul(): return jnp.dot(left, right, preferred_element_type=jnp.float32)  47.5 us
    dot_general x18, matrix products, inner_rows(): lax.dot_general(left, right, contract_rows, preferred_element_type=jnp.fl...  42.6 us
    psum x1, waiting for transfers between devices, body(): lax.psum(inner_cols(grad_pre, expand_proj).astype(jnp.bfloat16), 'tensor')  34.4 us
    reduce_scatter x1, waiting for transfers between devices, body(): lax.psum_scatter(join_heads(key_back).astype(jnp.bfloat16), 'ctx', scatte...  34.2 us
    psum x1, waiting for transfers between devices, body(): lax.psum(matmul(hidden, shrink_proj).astype(jnp.bfloat16), 'tensor')  34.2 us
    all_gather x1, waiting for transfers between devices, body(): lax.all_gather(values, 'ctx', axis=0, tiled=True)  31.5 us
  transfers between devices with their start and end apart: 10, of which 10 were waited for; matrix products, arithmetic and copies ran while one was open for 3% of the time, Pallas kernels for 0%

profile of v1, /device:TPU:0, one launch (start us, length us, event | category | flops | bytes accessed | tf_op | source)
XLA Modules:
  0.0 1210.5 jit_solution(13787616428495004286)
XLA Ops:
  7.3 2.8 convolution_convert_fusion.4
  10.2 2.4 fusion.62
  12.7 13.7 %all-gather = bf16[1,2048]{1,0:T(2,128)(2,1)S(1)} all-gather(bf16[1,512]{1,0:T(2,128)(2,1)S(1)} %get-tuple-element.303), channel_id=2, replica_groups=mesh['dp'=4,'ctx'=4,'tensor'=2] {'ctx'}, dimensions={1}, use_global_device_ids=true | all-gather | bytes 5120 | tf_op jit(solution)/shard_map/all_gather | solution.py:92
  29.1 21.0 %all-gather.4.cloned.1.call-done = bf16[2048,384]{1,0:T(8,128)(2,1)} async-done(((bf16[512,384]{1,0:T(8,128)(2,1)}), bf16[2048,384]{1,0:T(8,128)(2,1)}) %all-gather.4.cloned.1.call-update) | async-done | bytes 1572880 | tf_op jit(solution)/shard_map/all_gather | solution.py:90
  50.1 2.6 copy.43
  52.6 4.1 copy.45
  56.8 31.5 %all-gather.6.cloned.1.call-done = bf16[2048,384]{1,0:T(8,128)(2,1)} async-done(((bf16[512,384]{1,0:T(8,128)(2,1)}), bf16[2048,384]{1,0:T(8,128)(2,1)}) %all-gather.6.cloned.1.call-update) | async-done | bytes 1572880 | tf_op jit(solution)/shard_map/all_gather | solution.py:91
  88.2 2.6 copy.44
  90.8 4.1 copy.46
  94.9 38.4 %while.28 = (s32[]{:T(128)}, bf16[6,512,64]{1,2,0:T(8,128)(2,1)S(1)}, f32[6,512,1]{1,2,0:T(1,128)}, bf16[6,512,64]{2,1,0:T(8,128)(2,1)}, bf16[6,2048,64]{2,1,0:T...) while((s32[]{:T(128)}, ...), condition=%wide.region_3.4_spmd.clone, body=%wide.region_0.3_spmd.clone.sunk | while | flops 286260736 | bytes 13946985 | solution.py:119
  98.1 2.6 fusion.134
  104.5 2.6 fusion.134
  110.9 2.6 fusion.134
  117.3 2.6 fusion.134
  123.7 2.6 fusion.134
  130.1 2.6 fusion.134
  133.3 2.7 convolution_convert_fusion.2
  140.6 28.8 %all-reduce.11.cloned.1.call-done = bf16[512,768]{1,0:T(8,128)(2,1)} async-done(((bf16[512,768]{1,0:T(8,128)(2,1)}), bf16[512,768]{1,0:T(8,128)(2,1)}) %all-reduce.11.cloned.1.call-update) | async-done | bytes 786448 | tf_op jit(solution)/shard_map/psum | solution.py:121
  171.5 9.5 multiply_convert_fusion.1
  182.2 2.3 convolution_convert_fusion.1
  184.8 34.2 %all-reduce.13.cloned.1.call-done = bf16[512,768]{1,0:T(8,128)(2,1)} async-done(((bf16[512,768]{1,0:T(8,128)(2,1)}), bf16[512,768]{1,0:T(8,128)(2,1)}) %all-reduce.13.cloned.1.call-update) | async-done | bytes 786448 | tf_op jit(solution)/shard_map/psum | solution.py:134
  225.0 2.9 convert_reduce_fusion
  229.1 2.3 convolution_convert_fusion
  231.5 34.4 %all-reduce.15.cloned.1.call-done = bf16[512,768]{1,0:T(8,128)(2,1)} async-done(((bf16[512,768]{1,0:T(8,128)(2,1)}), bf16[512,768]{1,0:T(8,128)(2,1)}) %all-reduce.15.cloned.1.call-update) | async-done | bytes 786448 | tf_op jit(solution)/shard_map/psum | solution.py:153
  265.9 3.5 multiply_reduce_fusion.1
  273.7 69.9 %while.29 = (s32[]{:T(128)}, bf16[6,512,64]{1,2,0:T(8,128)(2,1)S(1)}, bf16[6,2048,64]{1,2,0:T(8,128)(2,1)}, bf16[6,2048,64]{1,2,0:T(8,128)(2,1)}, bf16[6,512,64]...) while((s32[]{:T(128)}, ...), condition=%wide.region_17.18_spmd.clone, body=%wide.region_15.17_spmd.clone.sunk | while | flops 681737728 | bytes 34759808 | solution.py:177
  276.2 2.6 multiply_reduce_fusion.7
  287.8 2.6 multiply_reduce_fusion.7
  299.5 2.6 multiply_reduce_fusion.7
  311.1 2.6 multiply_reduce_fusion.7
  322.8 2.6 multiply_reduce_fusion.7
  334.4 2.6 multiply_reduce_fusion.7
  345.0 5.1 fusion.67
  350.2 3.8 fusion.73
  357.2 21.8 %reduce-scatter.5.cloned.1.call-done = bf16[512,384]{0,1:T(8,128)(2,1)} async-done(((bf16[2048,384]{0,1:T(8,128)(2,1)}), bf16[512,384]{0,1:T(8,128)(2,1)}) %reduce-scatter.5.cloned.1.call-update) | async-done | bytes 393232 | tf_op jit(solution)/shard_map/reduce_scatter | solution.py:185
  379.0 2.5 convolution_bitcast_fusion.1
  381.5 34.2 %reduce-scatter.3.cloned.1.call-done = bf16[512,384]{0,1:T(8,128)(2,1)} async-done(((bf16[2048,384]{0,1:T(8,128)(2,1)}), bf16[512,384]{0,1:T(8,128)(2,1)}) %reduce-scatter.3.cloned.1.call-update) | async-done | bytes 393232 | tf_op jit(solution)/shard_map/reduce_scatter | solution.py:182
  415.8 2.5 convolution_bitcast_fusion.2
  422.4 477.3 %all-reduce.19.cloned.1.call-done = (f32[768,384]{0,1:T(8,128)}, f32[768,384]{0,1:T(8,128)}, f32[768,384]{0,1:T(8,128)}, f32[384,768]{1,0:T(8,128)}, f32[768,1536]{1,0:T(8,128)}, /*index=5*/f32[1536,768]{1,0:T(8,128)}) async-done(((f32[768,384]{0,1:T(8,128)}, f32[768,384]{0,1:T(8,128)}, f32[768,384]{0,1:T(8,128)}, f32[384,768]{1,0:T(8,128)}, f32[768,1536]{1,0:T(8,128)}, /*index=5*/f32[1536,768]{1,0:T(8,128)}), ...) | async-done | bytes 14155792 | tf_op jit(solution)/shard_map/psum | solution.py:15
  900.9 17.3 %all-reduce = (f32[384]{0:T(512)S(1)}, f32[384]{0:T(512)S(1)}, f32[768]{0:T(1024)S(1)}, f32[768]{0:T(1024)S(1)}, f32[768]{0:T(1024)S(1)}, /*index=5*/f32[1536]{0...) all-reduce(f32[384]{0:T(512)S(1)} %reduce_sum.182, ...), channel_id=1, replica_groups=mesh['dp'=4,'ctx'=4,'tensor'=2] {'ctx'}, use_global_device_ids=true, to_apply=%region_28.29 | all-reduce | flops 6912 | bytes 55296 | tf_op jit(solution)/shard_map/psum | solution.py:15
  918.2 11.1 all-reduce.2
  929.3 6.7 all-reduce.17.cloned.1.call-done
  935.9 2.4 convert_add_fusion
  938.4 248.5 %all-reduce.21.cloned.1.call-done = (f32[768,384]{0,1:T(8,128)}, f32[768,384]{0,1:T(8,128)}, f32[768,384]{0,1:T(8,128)}, f32[384,768]{1,0:T(8,128)}, f32[768,1536]{1,0:T(8,128)}, /*index=5*/f32[1536,768]{1,0:T(8,128)}) async-done(((f32[768,384]{0,1:T(8,128)}, f32[768,384]{0,1:T(8,128)}, f32[768,384]{0,1:T(8,128)}, f32[384,768]{1,0:T(8,128)}, f32[768,1536]{1,0:T(8,128)}, /*index=5*/f32[1536,768]{1,0:T(8,128)}), ...) | async-done | bytes 14155792 | tf_op jit(solution)/shard_map/psum | solution.py:15
  1186.8 2.7 copy.50
  1189.6 2.7 copy.51
  1194.7 5.5 copy.98
  1200.3 2.4 copy.99
  (241 shorter events, 112.4 us)
Async XLA Ops:
  7.2 164.2 %copy-start = (bf16[768,1536]{1,0:T(8,128)(2,1)S(1)}, bf16[768,1536]{1,0:T(8,128)(2,1)}, u32[]{:S(2)}) copy-start(bf16[768,1536]{1,0:T(8,128)(2,1)} %param.33) | copy-start | bytes 7077892
  7.2 3.0 copy-start.2
  7.2 2.9 copy-start.48
  7.2 5.4 copy-start.49
  7.2 5.4 copy-start.44
  7.2 42.8 %all-gather.4.cloned.1.call-start = ((), (), s32[]{:S(2)}) async-start(), calls=%async_computation.2 | async-start | bytes 1966080 | tf_op jit(solution)/shard_map/all_gather | solution.py:90
  10.1 78.1 %all-gather.6.cloned.1.call-start = ((), (), s32[]{:S(2)}) async-start(), calls=%async_computation.3 | async-start | bytes 1966080 | tf_op jit(solution)/shard_map/all_gather | solution.py:91
  12.6 156.8 %all-reduce.11.cloned.1.call-start = ((), (), s32[]{:S(2)}) async-start(), calls=%async_computation.4 | async-start | bytes 1572864 | tf_op jit(solution)/shard_map/psum | solution.py:121
  133.3 38.1 %copy-start.13 = (bf16[6,512,64]{1,2,0:T(8,128)(2,1)}, bf16[6,512,64]{1,2,0:T(8,128)(2,1)S(1)}, u32[]{:S(2)}) copy-start(bf16[6,512,64]{1,2,0:T(8,128)(2,1)S(1)} %get-tuple-element.109) | copy-start | bytes 1179652
  136.0 83.0 %all-reduce.13.cloned.1.call-start = ((), (), s32[]{:S(2)}) async-start(), calls=%async_computation.5 | async-start | bytes 1572864 | tf_op jit(solution)/shard_map/psum | solution.py:134
  169.4 2.1 copy-start.42
  170.9 10.1 copy-start.27
  171.5 9.5 copy-start.30
  171.5 10.7 copy-start.50
  182.2 2.6 copy-start.45
  182.2 2.6 copy-start.46
  182.2 2.6 copy-start.47
  182.2 36.8 %copy-start.25 = (f32[768]{0:T(1024)S(1)}, f32[768]{0:T(1024)}, u32[]{:S(2)}) copy-start(f32[768]{0:T(1024)} %convert_element_type.185) | copy-start | bytes 9220
  182.2 36.8 %copy-start.28 = (f32[512]{0:T(512)S(1)}, f32[512]{0:T(512)}, u32[]{:S(2)}) copy-start(f32[512]{0:T(512)} %copy-done.27) | copy-start | bytes 6148
  182.2 36.8 %copy-start.31 = (f32[512]{0:T(512)S(1)}, f32[512]{0:T(512)}, u32[]{:S(2)}) copy-start(f32[512]{0:T(512)} %copy-done.30) | copy-start | bytes 6148
  182.2 36.8 %copy-start.40 = (f32[768]{0:T(1024)S(1)}, f32[768]{0:T(1024)}, u32[]{:S(2)}) copy-start(f32[768]{0:T(1024)} %convert_element_type.186) | copy-start | bytes 9220
  184.5 81.4 %all-reduce.15.cloned.1.call-start = ((), (), s32[]{:S(2)}) async-start(), calls=%async_computation.6 | async-start | bytes 1572864 | tf_op jit(solution)/shard_map/psum | solution.py:153
  219.0 2.6 copy-start.15
  221.3 3.4 copy-start.55
  221.6 3.1 copy-start.54
  224.7 3.2 copy-start.3
  231.4 38.0 %copy-start.4 = (f32[512,768]{1,0:T(8,128)S(1)}, f32[512,768]{1,0:T(8,128)}, u32[]{:S(2)}) copy-start(f32[512,768]{1,0:T(8,128)} %copy-done.3) | copy-start | bytes 4718596
  231.4 38.0 %copy-start.9 = (bf16[512,768]{1,0:T(8,128)(2,1)S(1)}, bf16[512,768]{1,0:T(8,128)(2,1)}, u32[]{:S(2)}) copy-start(bf16[512,768]{1,0:T(8,128)(2,1)} %all-reduce.11.cloned.1.call-done) | copy-start | bytes 2359300
  231.4 147.6 %reduce-scatter.5.cloned.1.call-start = ((), (), s32[]{:S(2)}) async-start(), calls=%async_computation.8 | async-start | bytes 1966080 | tf_op jit(solution)/shard_map/reduce_scatter | solution.py:185
  265.9 3.6 copy-start.16
  269.4 2.5 copy-start.18
  343.6 72.2 %reduce-scatter.3.cloned.1.call-start = ((), (), s32[]{:S(2)}) async-start(), calls=%async_computation.7 | async-start | bytes 1966080 | tf_op jit(solution)/shard_map/reduce_scatter | solution.py:182
  344.4 5.8 copy-start.10
  344.4 5.8 copy-start.26
  344.4 5.8 copy-start.29
  344.4 5.7 copy-start.32
  344.4 555.3 %all-reduce.19.cloned.1.call-start = ((), (), s32[]{:S(2)}) async-start(), calls=%async_computation.10 | async-start | bytes 28311552 | tf_op jit(solution)/shard_map/psum | solution.py:15
  345.0 5.2 copy-start.41
  345.0 5.2 copy-start.53
  418.3 517.7 %all-reduce.17.cloned.1.call-start = ((), (), s32[]{:S(2)}) async-start(), calls=%async_computation.9 | async-start | bytes 1572864 | tf_op jit(solution)/shard_map/psum | solution.py:201
  418.3 2.5 copy-start.11
  418.3 2.5 copy-start.22
  422.4 764.5 %all-reduce.21.cloned.1.call-start = ((), (), s32[]{:S(2)}) async-start(), calls=%async_computation.11 | async-start | bytes 28311552 | tf_op jit(solution)/shard_map/psum | solution.py:15
  1186.8 5.5 copy-start.21
  1189.6 4.1 copy-start.20
  1193.7 6.5 slice-start
  1194.7 5.5 slice-start.1
  1200.3 3.4 copy-start.1
  (20 other events, 28.6 us)
Sparse Core Ops, SparseCore 0:
  10.2 39.8 all-gather.3
  52.2 35.9 all-gather.5
  136.1 33.1 all-reduce.10
  184.6 34.3 all-reduce.12
  231.5 34.2 all-reduce.14
  343.7 35.2 reduce-scatter.4
  381.4 34.2 reduce-scatter.2
  420.5 479.1 all-reduce.18
  902.7 33.2 all-reduce.16
  938.9 247.8 all-reduce.20
